TPU v7x, 128 devices: a whole 4x4x4 slice. The times are simulated.
128 devices in a mesh: px: 8 (over x, core), py: 16 (over z, y).
Axes of the slice: x: 4, y: 4, z: 4, core: 2. Of those that a mesh axis runs over, the one named last changes fastest.
Arguments:
- fields: float32 [4, 35, 589824], P(None, None, ('px', 'py')), may hold values from -6 to 6
- residue: float32 [4, 35, 589824], P(None, None, ('px', 'py')), may hold values from -4 to 4
- geometry: float32 [9, 589824], P(None, ('px', 'py')), may hold values from -4 to 4
- normals: float32 [3, 4, 589824], P(None, None, ('px', 'py')), as said below
- face_scale: float32 [4, 589824], P(None, ('px', 'py')), may hold values from 0.5 to 4
- neighbours: int32 [4, 589824], P(None, ('px', 'py')), may hold values from -1 to 19199, as said below
- send_faces: int32 [8, 12288], P(None, ('px', 'py')), may hold values from 0 to 14591, as said below
- live_counts: int32 [128], P(('px', 'py')), may hold values from 768 to 4608, as said below
- sample_ids: int32 [25600], P(('px', 'py')), may hold values from 0 to 25599, each once
- sample_elems: int32 [25600], P(('px', 'py')), may hold values from 0 to 4607, as said below
- sample_coords: float32 [3, 25600], P(None, ('px', 'py')), as said below
Outputs:
- fields_next: float32 [4, 35, 589824], P(None, None, ('px', 'py'))
- residue_next: float32 [4, 35, 589824], P(None, None, ('px', 'py'))
- coefficients: float32 [25, 512], P(None, ('px', 'py'))
Inputs may be any that keep to these rules, and one draw needn't show every extreme that they name: `live_counts`: one partition holds exactly 4608 live slots, each other one between 768 and 2304. `neighbours`: codes of live slots name live face blocks. Slot d * 96 + j, for d below 8, has exactly one face coded 4 * 4608 + d * 96 + j, or coded -1 where that neighbour lies off the grid; no other face has a code at or above 18432. Matched faces list their nodes in the same order. send_faces[d, P * 96 + j] is the face block of partition P's slot d * 96 + j that faces neighbour d. `sample_elems`: each names a live slot of the partition holding the sample slot. `sample_coords`: the point lies inside the reference tetrahedron. `normals`: unit vectors.
All inputs are finite; a program needn't handle non-finite values.
Results may differ from a plain program's by a relative error of at most 0.0003.
Values sent between devices are 32-bit elements; how exact they have to be, the bound alone decides.
No kernel may reach another device: no remote copies, remote signals or barrier semaphores. Data moves between devices by JAX's collectives and lax.ppermute only.
A program may use at most 128 MiB of HBM per device.

v0:
```python
import functools
import math

import jax
import jax.numpy as jnp
import numpy as np
from jax import lax
from jax.experimental import pallas as pl
from jax.experimental.pallas import tpu as pltpu
from jax.sharding import PartitionSpec as P

QPTS = 50
NODES = 35
PAD = 40
FACE_ROWS = 16
ROWS = 144
LANES = 128
FACE_TILES = 4


highest = lax.Precision.HIGHEST
section_decay = -567301805773.0 / 1357537059087.0
section_gain = 5161836677717.0 / 13612068292357.0
time_step = 0.01
f32 = jnp.float32
bf16 = jnp.bfloat16


def exponent_table():
    listing = []
    for degree in range(5):
        for third in range(degree + 1):
            for second in range(degree + 1 - third):
                listing.append((degree - second - third, second, third))
    return np.array(listing)


def factorials(values):
    lookup = np.array([float(math.factorial(level)) for level in range(24)])
    return lookup[values]


def eliminate(matrix, right_hand):
    order_size = matrix.shape[0]
    work = np.concatenate([matrix, right_hand], axis=1).astype(float)
    for pivot_col in range(order_size):
        best = max(range(pivot_col, order_size), key=lambda row_id: abs(work[row_id, pivot_col]))
        work[[pivot_col, best]] = work[[best, pivot_col]]
        work[pivot_col] = work[pivot_col] / work[pivot_col, pivot_col]
        for row_id in range(order_size):
            if row_id != pivot_col:
                work[row_id] = work[row_id] - work[row_id, pivot_col] * work[pivot_col]
    return work[:, order_size:]


def element_tables():
    powers = exponent_table()
    points = powers / 4.0
    vander = np.prod(points[:, None, :] ** powers[None, :, :], axis=2)
    inverse = eliminate(vander, np.eye(35))
    derivs = []
    for axis_id in range(3):
        lowered = np.maximum(powers - (np.arange(3) == axis_id)[None, :], 0)
        slope_table = powers[None, :, axis_id] * np.prod(
            points[:, None, :] ** lowered[None, :, :], axis=2
        )
        derivs.append(slope_table @ inverse)
    summed = powers[:, None, :] + powers[None, :, :]
    exp_r = summed[..., 0]
    exp_s = summed[..., 1]
    exp_t = summed[..., 2]
    volume = (
        factorials(exp_r)
        * factorials(exp_s)
        * factorials(exp_t)
        / factorials(exp_r + exp_s + exp_t + 3)
    )
    mass_matrix = inverse.T @ volume @ inverse
    face_grams = [
        np.where(
            exp_t == 0, factorials(exp_r) * factorials(exp_s) / factorials(exp_r + exp_s + 2), 0.0
        ),
        np.where(
            exp_s == 0, factorials(exp_r) * factorials(exp_t) / factorials(exp_r + exp_t + 2), 0.0
        ),
        factorials(exp_r)
        * factorials(exp_s)
        * factorials(exp_t)
        / factorials(exp_r + exp_s + exp_t + 2),
        np.where(
            exp_r == 0, factorials(exp_s) * factorials(exp_t) / factorials(exp_s + exp_t + 2), 0.0
        ),
    ]
    listed = [tuple((int(entry) for entry in powers[node_id])) for node_id in range(35)]
    face_nodes = np.array(
        [
            [node_id for node_id in range(35) if listed[node_id][2] == 0],
            [node_id for node_id in range(35) if listed[node_id][1] == 0],
            [node_id for node_id in range(35) if sum(listed[node_id]) == 4],
            [node_id for node_id in range(35) if listed[node_id][0] == 0],
        ]
    )
    surface = np.zeros((35, 60))
    for face_id in range(4):
        face_mass = inverse.T @ face_grams[face_id] @ inverse
        for node_id in range(15):
            surface[:, 4 * node_id + face_id] = face_mass[:, face_nodes[face_id, node_id]]
    lifting = eliminate(mass_matrix, surface)
    return (np.stack(derivs), lifting, face_nodes, inverse, powers)


def associated(degree, order, cosine, sine):
    current = cosine * 0.0 + 1.0
    for step_id in range(1, order + 1):
        current = -(2 * step_id - 1) * sine * current
    if degree == order:
        return current
    following = cosine * (2 * order + 1) * current
    for level in range(order + 2, degree + 1):
        current, following = (
            following,
            ((2 * level - 1) * cosine * following - (level + order - 1) * current)
            / (level - order),
        )
    return following


def harmonic_table():
    inner_node = math.sqrt(5.0 - 2.0 * math.sqrt(10.0 / 7.0)) / 3.0
    outer_node = math.sqrt(5.0 + 2.0 * math.sqrt(10.0 / 7.0)) / 3.0
    inner_weight = (322.0 + 13.0 * math.sqrt(70.0)) / 900.0
    outer_weight = (322.0 - 13.0 * math.sqrt(70.0)) / 900.0
    cosines = np.array([-outer_node, -inner_node, 0.0, inner_node, outer_node])
    weights = np.array([outer_weight, inner_weight, 128.0 / 225.0, inner_weight, outer_weight])
    azimuth = 2.0 * np.pi * (np.arange(10) + 0.5) / 10.0
    polar = np.repeat(cosines, 10)
    circle = np.tile(azimuth, 5)
    point_weight = np.repeat(weights, 10) * 2.0 * np.pi / 10.0
    sine = np.sqrt(1.0 - polar**2)
    table_rows = []
    for degree in range(5):
        for order in range(-degree, degree + 1):
            absolute = abs(order)
            legendre = associated(degree, absolute, polar, sine)
            factor = math.sqrt(
                (2 * degree + 1)
                / (4.0 * math.pi)
                * math.factorial(degree - absolute)
                / math.factorial(degree + absolute)
            )
            if order > 0:
                angular = math.sqrt(2.0) * np.cos(order * circle)
            elif order < 0:
                angular = math.sqrt(2.0) * np.sin(absolute * circle)
            else:
                angular = circle * 0.0 + 1.0
            table_rows.append(factor * legendre * angular * point_weight)
    return np.array(table_rows)


def constant_tables():
    derivs, lifting, face_nodes, inverse, powers = element_tables()
    table_select = np.zeros((ROWS, 4 * LANES), np.float32)
    trace_select = np.zeros((4 * 4 * FACE_ROWS, ROWS), np.float32)
    for face in range(4):
        for field in range(4):
            for place in range(15):
                source = 4 * face_nodes[face, place] + field
                column = FACE_ROWS * field + place
                table_select[source, LANES * face + column] = 1.0
                table_select[source, LANES * face + 64 + column] = 1.0
                trace_select[64 * face + column, source] = 1.0
    whole = np.round(3.0 * derivs)
    into_p = np.zeros((ROWS, 128), np.float32)
    from_p = np.zeros((3 * ROWS, 48), np.float32)
    lift = np.zeros((ROWS, 256), np.float32)
    for node in range(NODES):
        for axis_id in range(3):
            into_p[4 * node, PAD * axis_id : PAD * axis_id + NODES] = -whole[axis_id, node]
            for field in range(1, 4):
                from_p[ROWS * axis_id + 4 * node + field, :NODES] = whole[axis_id, node]
        for face in range(4):
            for place in range(15):
                entry = lifting[node, 4 * place + face]
                column = FACE_ROWS * face + place
                lift[4 * node, column] = entry
                for field in range(1, 4):
                    lift[4 * node + field, 64 * field + column] = -entry
    lift_hi = lift.astype(jnp.bfloat16)
    lift_lo = (lift - lift_hi.astype(np.float32)).astype(jnp.bfloat16)
    return {
        "table_select": jnp.asarray(np.concatenate([table_select] * 2, axis=0), bf16),
        "trace_select": jnp.asarray(trace_select, bf16),
        "twice_select": jnp.asarray(np.concatenate([trace_select] * 2, axis=1), bf16),
        "from_p": jnp.asarray(np.concatenate([from_p, from_p], axis=1), bf16),
        "lift": jnp.asarray(
            np.concatenate(
                [lift_hi, lift_lo, lift_hi] + [into_p.astype(jnp.bfloat16)] * 2, axis=1
            )
        ),
        "inverse": jnp.asarray(np.pad(inverse.T, ((0, 5), (0, 5))), f32),
        "powers": powers,
    }


def halves(values):
    high = values.astype(bf16)
    return high, (values - high.astype(f32)).astype(bf16)


def thirds(values):
    high = values.astype(bf16)
    rest = values - high.astype(f32)
    middle = rest.astype(bf16)
    return high, middle, (rest - middle.astype(f32)).astype(bf16)


def product(left, right, dims=((1,), (0,))):
    return lax.dot_general(left, right, (dims, ((), ())), preferred_element_type=f32)


def stack_nodes(fields_ref, stacked):
    tiles = range(stacked.shape[0])
    for tile in tiles:
        for node in range(NODES):
            stacked[tile, 4 * node : 4 * node + 4, :] = fields_ref[
                node, :, LANES * tile : LANES * tile + LANES
            ]
    return halves(jnp.concatenate([stacked[tile] for tile in tiles], axis=1))


def one_field(stacked, field):
    tiles = range(stacked.shape[0])
    rows = pl.ds(field, NODES, stride=4)
    return jnp.concatenate([stacked[tile, rows, :] for tile in tiles], axis=1)


def pack_kernel(
    slot_faces,
    fields_ref,
    codes_ref,
    select_ref,
    up_ref,
    down_ref,
    left_ref,
    right_ref,
    faces_ref,
    stacked,
):
    stacked[...] = jnp.zeros_like(stacked)
    high, low = stack_nodes(fields_ref, stacked)
    traces = product(select_ref[...], high) + product(select_ref[...], low)
    reach = fields_ref.shape[2]
    count = reach // 8
    chosen = jnp.zeros((64, reach), f32)
    for face in range(4):
        remote = codes_ref[face : face + 1, 0:reach] >= slot_faces
        chosen = jnp.where(remote, traces[64 * face : 64 * face + 64, :], chosen)
    homes = [up_ref.at[0], up_ref.at[1], up_ref.at[2], left_ref, right_ref]
    homes += [down_ref.at[0], down_ref.at[1], down_ref.at[2]]
    for heading, home in enumerate(homes):
        part = chosen[:, count * heading : count * heading + count]
        home[:, 0:96] = part[0:48]
        for third in range(3):
            home[16 * third : 16 * third + 16, 96:128] = part[48:64, 32 * third : 32 * third + 32]
    tiles = codes_ref.shape[1] // LANES
    codes = codes_ref[...]
    codes = jnp.where((codes >= 0) & (codes < slot_faces), codes, 0)
    for face in range(4):
        for tile in range(tiles):
            row = 4 * FACE_TILES * (tile // FACE_TILES) + FACE_TILES * face + tile % FACE_TILES
            faces_ref[row : row + 1, :] = codes[
                face : face + 1, LANES * tile : LANES * tile + LANES
            ]


def relay_kernel(left_ref, right_ref, below_ref, above_ref, to_left_ref, to_right_ref):
    to_left_ref[0] = left_ref[...]
    to_left_ref[1] = below_ref[0]
    to_left_ref[2] = above_ref[0]
    to_right_ref[0] = right_ref[...]
    to_right_ref[1] = below_ref[2]
    to_right_ref[2] = above_ref[2]


def build_rows(first, part, fields_ref, select_ref, table_ref, stacked):
    slot_count = table_ref.shape[0] // 4
    width = LANES * stacked.shape[0]
    high, low = stack_nodes(fields_ref.at[:, :, width * part : width * part + width], stacked)
    both = jnp.concatenate([high, low], axis=0)
    for half in range(2):
        select = select_ref[:, 256 * half : 256 * half + 256]
        rows = product(both, select, ((0,), (0,)))
        for side in range(2):
            start = pl.multiple_of((2 * half + side) * slot_count + first + width * part, width)
            table_ref[pl.ds(start, width), :] = rows[:, LANES * side : LANES * side + LANES]


def gather_pieces(faces_ref, table_ref, normals_ref, outer_ref, rows_refs):
    width = outer_ref.shape[1]
    left_half = lax.broadcasted_iota(jnp.int32, (1, LANES), 1) < 64

    def load(tile, rows):
        for row in rows:
            at = tile * LANES + row
            for half in range(2):
                one = table_ref[pl.ds(faces_ref[2 * half * width + at], 1), :]
                two = table_ref[pl.ds(faces_ref[(2 * half + 1) * width + at], 1), :]
                rows_ref = rows_refs[2 * (tile % 2) + half]
                rows_ref[row : row + 1, :] = jnp.where(left_half, one, two)

    def combine(tile, half):
        turned = rows_refs[2 * (tile % 2) + half][...].T
        lanes = slice(tile * LANES, tile * LANES + LANES)
        for side in range(2):
            face = 2 * half + side
            part = turned[64 * side : 64 * side + 64, :]
            total = -part[0:16]
            for axis_id in range(3):
                facing = normals_ref[axis_id, face : face + 1, lanes]
                total = total + facing * part[16 + 16 * axis_id : 32 + 16 * axis_id]
            outer_ref[FACE_ROWS * face : FACE_ROWS * face + FACE_ROWS, lanes] = total

    for tile in range(width // LANES):
        for part in range(8):
            rows = range(16 * part, 16 * part + 16)
            yield functools.partial(load, tile, rows)
            if tile > 0 and part < 2:
                yield functools.partial(combine, tile - 1, part)
    for half in range(2):
        yield functools.partial(combine, tile, half)


def section_kernel(
    slot_count,
    reach,
    live_ref,
    faces_hbm,
    next_normals_ref,
    bulk_ref,
    fields_ref,
    residue_ref,
    geometry_ref,
    normals_ref,
    scale_ref,
    codes_ref,
    elems_ref,
    table_select_ref,
    select_ref,
    from_ref,
    lift_ref,
    fields_out,
    residue_out,
    sampled,
    table_ref,
    stacked,
    combined,
    slow,
    rates,
    outer,
    beyond_ref,
    pressure,
    fields_split,
    slow_split,
    inner,
    sources,
    even_faces,
    odd_faces,
    arrived,
    *rows_refs,
):
    faces_refs = (even_faces, odd_faces)
    width = fields_ref.shape[2]
    tiles = slot_count // width
    bulks = slot_count // bulk_ref.shape[2]
    step = pl.program_id(0) - bulks
    slot_faces = 4 * slot_count
    half_width = 256

    def codes_copy(tile, parity):
        source = faces_hbm.at[pl.ds(pl.multiple_of(tile * 4 * width, 4 * width), 4 * width)]
        return pltpu.make_async_copy(source, faces_refs[parity], arrived.at[parity])

    def gather(parity):
        return gather_pieces(
            faces_refs[parity], table_ref, next_normals_ref, outer, rows_refs
        )

    def take_codes(parity):
        codes_copy(step, parity).wait()

        @pl.when((step + 1) * width < live_ref[0])
        def _():
            codes_copy(step + 1, 1 - parity).start()

    def update_pieces():
        first = (step - 1) * width

        def stack(at, low, high):
            for tile in range(2 * at, 2 * at + 2):
                for node in range(low, high):
                    stacked[tile, 4 * node : 4 * node + 4, :] = fields_ref[
                        node, :, LANES * tile : LANES * tile + LANES
                    ]

        def split(at):
            for side in range(2):
                lanes = slice(LANES * side, LANES * side + LANES)
                high, low = halves(stacked[2 * at + side])
                fields_split[at, 0:ROWS, lanes] = high
                fields_split[at, ROWS : 2 * ROWS, lanes] = low

        def inside(at):
            return slice(half_width * at, half_width * at + half_width)

        def field_rows(at, field):
            rows = pl.ds(field, NODES, stride=4)
            return jnp.concatenate([stacked[tile, rows, :] for tile in (2 * at, 2 * at + 1)], axis=1)

        def copy_slow(at):
            lanes = inside(at)
            slow[0:NODES, lanes] = field_rows(at, 0)
            slow_split[at, 0:48, :], slow_split[at, 48:96, :] = halves(slow[:, lanes])

        def weigh(at, axis_id):
            lanes = inside(at)
            weighted = jnp.zeros((NODES, half_width), f32)
            for direction in range(3):
                row = 3 * axis_id + direction
                factor = geometry_ref[row : row + 1, lanes] * (1.0 / 3.0)
                weighted = weighted + factor * field_rows(at, 1 + direction)
            combined[PAD * axis_id : PAD * axis_id + NODES, lanes] = weighted

        def split_weighted(at):
            high, low = halves(combined[:, inside(at)])
            sources[at, 768:896, :], sources[at, 896:1024, :] = high, low

        def traces(at):
            inner[at] = product(select_ref[...], fields_split[at])

        def slope(at, axis_id):
            lanes = inside(at)
            place = lax.broadcasted_iota(jnp.int32, (8, half_width), 0) & 3
            value = product(from_ref[ROWS * axis_id : ROWS * axis_id + ROWS, :], slow_split[at])
            pattern = jnp.zeros((8, half_width), f32)
            for direction in range(3):
                row = 3 * axis_id + direction
                factor = geometry_ref[row : row + 1, lanes] * (1.0 / 3.0)
                pattern = jnp.where(place == direction + 1, factor, pattern)
            value = value.reshape(ROWS // 8, 8, half_width) * pattern[None]
            value = value.reshape(ROWS, half_width)
            if axis_id == 0:
                rates[:, lanes] = value
            else:
                rates[:, lanes] += value

        def keep_split(at, start, value):
            high, low = halves(value)
            rows = value.shape[0]
            sources[at, start : start + rows, :] = high
            sources[at, 256 + start : 256 + start + rows, :] = high
            sources[at, 512 + start : 512 + start + rows, :] = low

        def jump(at, face):
            lanes = inside(at)
            inner_p = inner[at, 64 * face : 64 * face + 16, :]
            along = jnp.zeros_like(inner_p)
            for axis_id in range(3):
                facing = normals_ref[axis_id, face : face + 1, lanes]
                start = 64 * face + 16 + 16 * axis_id
                along = along + facing * inner[at, start : start + 16, :]
            wall = codes_ref[face : face + 1, lanes] < 0
            beyond = beyond_ref[FACE_ROWS * face : FACE_ROWS * face + FACE_ROWS, lanes]
            beyond = jnp.where(wall, -along - inner_p, beyond)
            beyond = jnp.where(codes_ref[face : face + 1, lanes] >= slot_faces, 0.0, beyond)
            scale = 0.5 * scale_ref[face : face + 1, lanes]
            value = scale * (along - inner_p - beyond)
            keep_split(at, FACE_ROWS * face, value)
            for axis_id in range(3):
                start = 64 + 64 * axis_id + FACE_ROWS * face
                keep_split(at, start, normals_ref[axis_id, face : face + 1, lanes] * value)

        def lift(at):
            lanes = inside(at)
            rates[:, lanes] = product(lift_ref[...], sources[at]) - rates[:, lanes]

        def advance(at, low, high):
            lanes = inside(at)
            slots = lax.broadcasted_iota(jnp.int32, (1, half_width), 1) + (first + half_width * at)
            keep = slots < live_ref[0]
            for node in range(low, high):
                rate = rates[4 * node : 4 * node + 4, lanes]
                residue_next = section_decay * residue_ref[node, :, lanes] + time_step * rate
                fields_next = fields_ref[node, :, lanes] + section_gain * residue_next
                fields_next = jnp.where(keep, fields_next, 0.0)
                fields_out[node, :, lanes] = fields_next
                residue_out[node, :, lanes] = jnp.where(keep, residue_next, 0.0)
                pressure[node : node + 1, lanes] = fields_next[0:1]

        def sample(at):
            lanes = inside(at)
            parts = jnp.concatenate(thirds(pressure[:, lanes]), axis=0)
            start = first + half_width * at
            slots = lax.broadcasted_iota(jnp.int32, (half_width, elems_ref.shape[1]), 0) + start
            elems = elems_ref[...]
            picks = (slots == elems) & (elems >= reach)
            sampled[...] += product(parts, jnp.where(picks, 1.0, 0.0).astype(bf16))

        call = functools.partial

        def stages(at):
            sevens = range(0, NODES, 7)
            return [
                [call(stack, at, low, low + 7) for low in sevens] + [call(split, at)],
                [call(copy_slow, at)]
                + [call(weigh, at, axis_id) for axis_id in range(3)]
                + [call(split_weighted, at), call(traces, at)],
                [call(slope, at, axis_id) for axis_id in range(3)],
                [call(jump, at, face) for face in range(4)],
                [call(lift, at)],
                [call(advance, at, low, low + 7) for low in sevens],
                [call(sample, at)],
            ]

        both = [stages(at) for at in range(width // half_width)]
        depth = len(both[0])
        return [
            [piece for lag, chain in enumerate(both) if 0 <= at - lag < depth for piece in chain[at - lag]]
            for at in range(depth + len(both) - 1)
        ]

    def interleave(gathers, groups):
        gathers = list(gathers)

        def run(at, updates, groups):
            @pl.when(live_ref[0] > at)
            def _():
                low = at * len(gathers) // len(groups)
                loads = gathers[low : (at + 1) * len(gathers) // len(groups)]
                order = [(place / len(loads), 0, place) for place in range(len(loads))]
                order += [((place + 1) / len(updates), 1, place) for place in range(len(updates))]
                for _, kind, place in sorted(order):
                    (loads, updates)[kind][place]()

        cuts = (0, 4, 8)
        groups = [sum(groups[low:high], []) for low, high in zip(cuts, cuts[1:])]
        for at, updates in enumerate(groups):
            run(at, updates, groups)

    @pl.when(step == -bulks)
    def _():
        stacked[...] = jnp.zeros_like(stacked)
        combined[...] = jnp.zeros_like(combined)
        slow[...] = jnp.zeros_like(slow)
        pressure[...] = jnp.zeros_like(pressure)
        sampled[...] = jnp.zeros_like(sampled)

    @pl.when(step < 0)
    def _():
        first = (step + bulks) * bulk_ref.shape[2]
        for part in range(bulk_ref.shape[2] // width):

            @pl.when(first + width * part < live_ref[0])
            def _():
                build_rows(first, part, bulk_ref, table_select_ref, table_ref, stacked)

    @pl.when(step == -1)
    def _():
        codes_copy(0, 0).start()

    @pl.when(step == 0)
    def _():
        take_codes(0)
        for piece in gather(0):
            piece()

    for parity in range(2):

        @pl.when((step > 0) & (step * width < live_ref[0]) & (step % 2 == parity))
        def _():
            take_codes(parity)
            beyond_ref[...] = outer[...]
            interleave(gather(parity), update_pieces())

    @pl.when((step > 0) & ((step - 1) * width >= live_ref[0]))
    def _():
        fields_out[...] = jnp.zeros_like(fields_out)
        residue_out[...] = jnp.zeros_like(residue_out)

    @pl.when((step > 0) & ((step - 1) * width < live_ref[0]) & (step * width >= live_ref[0]))
    def _():
        beyond_ref[...] = outer[...]
        for stage in update_pieces():
            for piece in stage:
                piece()


def boundary_kernel(
    slot_faces,
    powers,
    group,
    fields_ref,
    residue_ref,
    normals_ref,
    scale_ref,
    codes_ref,
    right_ref,
    left_ref,
    below_ref,
    above_ref,
    elems_ref,
    ids_ref,
    coords_ref,
    partial_ref,
    lift_ref,
    inverse_ref,
    fields_out,
    residue_out,
    spread_ref,
    remote,
    sources,
    rates,
    pressure,
    monomials,
):
    reach = fields_ref.shape[2]
    bound_count = reach // 8
    pressure[...] = jnp.zeros_like(pressure)
    monomials[...] = jnp.zeros_like(monomials)
    arrivals = [
        left_ref[2],
        above_ref[1],
        right_ref[2],
        left_ref[0],
        right_ref[0],
        left_ref[1],
        below_ref[1],
        right_ref[1],
    ]
    for heading, source in enumerate(arrivals):
        start = bound_count * heading
        remote[0:48, start : start + 96] = source[:, 0:96]
        for third in range(3):
            place = start + 32 * third
            remote[48:64, place : place + 32] = source[16 * third : 16 * third + 16, 96:128]

    def keep_split(start, value):
        high, low = halves(value)
        sources[start : start + FACE_ROWS, :] = high
        sources[256 + start : 256 + start + FACE_ROWS, :] = high
        sources[512 + start : 512 + start + FACE_ROWS, :] = low

    for face in range(4):
        beyond = -remote[0:16, :]
        for axis_id in range(3):
            facing = normals_ref[axis_id, face : face + 1, :]
            beyond = beyond + facing * remote[16 + 16 * axis_id : 32 + 16 * axis_id, :]
        is_remote = codes_ref[face : face + 1, :] >= slot_faces
        flux = jnp.where(is_remote, -0.5 * scale_ref[face : face + 1, :] * beyond, 0.0)
        keep_split(FACE_ROWS * face, flux)
        for axis_id in range(3):
            facing = normals_ref[axis_id, face : face + 1, :]
            keep_split(64 + 64 * axis_id + FACE_ROWS * face, facing * flux)
    rates[...] = time_step * product(lift_ref[:, 0:768], sources[...])
    for node in range(NODES):
        rate = rates[4 * node : 4 * node + 4, :]
        residue_out[node] = residue_ref[node] + rate
        fields_next = fields_ref[node] + section_gain * rate
        fields_out[node] = fields_next
        pressure[node : node + 1, :] = fields_next[0:1]
    parts = jnp.concatenate(thirds(pressure[...]), axis=0)
    slots = lax.broadcasted_iota(jnp.int32, (reach, elems_ref.shape[1]), 0)
    picks = jnp.where(slots == elems_ref[...], 1.0, 0.0).astype(bf16)
    sampled = partial_ref[...] + product(parts, picks)
    ladders = []
    for axis_id in range(3):
        base = coords_ref[axis_id : axis_id + 1, :]
        square = base * base
        ladders.append([jnp.ones_like(base), base, square, square * base, square * square])
    for node in range(NODES):
        exps = [int(entry) for entry in powers[node]]
        monomials[node : node + 1, :] = (
            ladders[0][exps[0]] * ladders[1][exps[1]] * ladders[2][exps[2]]
        )
    basis = jnp.dot(
        inverse_ref[...], monomials[...], precision=highest, preferred_element_type=f32
    )
    gathered = sampled[0:PAD, :] + sampled[48 : 48 + PAD, :] + sampled[96 : 96 + PAD, :]
    values = jnp.sum(basis * gathered, axis=0, keepdims=True)
    ids = ids_ref[...]
    owner = lax.shift_right_logical(ids * 5243, 20)
    place = ids - group * owner
    owners = lax.broadcasted_iota(jnp.int32, (spread_ref.shape[0], ids.shape[1]), 0)
    held = jnp.where(owners == owner, values, 0.0)
    places = lax.broadcasted_iota(jnp.int32, (spread_ref.shape[2], ids.shape[1]), 0)
    chosen = jnp.where(places == place, 1.0, 0.0).astype(bf16)
    spread = jnp.zeros((spread_ref.shape[0], spread_ref.shape[2]), f32)
    for part in thirds(held):
        spread = spread + product(part, chosen, ((1,), (1,)))
    spread_ref[:, 0, :] = spread


def harmonic_kernel(received_ref, table_ref, groups_ref, out_ref):
    mine = jnp.sum(received_ref[...], axis=0)
    weighted = groups_ref[...] * mine
    out_ref[...] = lax.dot_general(
        weighted,
        table_ref[...],
        (((1,), (1,)), ((), ())),
        precision=highest,
        preferred_element_type=f32,
    )


def in_hbm(array):
    return pltpu.with_memory_space_constraint(array, pltpu.HBM)


def in_vmem(array):
    return pltpu.with_memory_space_constraint(array, pltpu.VMEM)


def fixed(shape):
    return pl.BlockSpec(shape, lambda *_: (0,) * len(shape))


def local(
    fields,
    residue,
    geometry,
    normals,
    face_scale,
    neighbours,
    send_faces,
    live_counts,
    sample_ids,
    sample_elems,
    sample_coords,
):
    const = {
        name: in_hbm(table) if isinstance(table, jax.Array) else table
        for name, table in constant_tables().items()
    }
    fields = in_hbm(jnp.transpose(fields, (1, 0, 2)))
    residue = in_hbm(jnp.transpose(residue, (1, 0, 2)))
    geometry, normals, face_scale = in_hbm(geometry), in_hbm(normals), in_hbm(face_scale)
    neighbours, sample_coords = in_hbm(neighbours), in_hbm(sample_coords)
    slot_count = fields.shape[2]
    slot_faces = 4 * slot_count
    bound_count = send_faces.shape[1]
    reach = 8 * bound_count
    samples = sample_ids.shape[0]
    devices = lax.axis_size(("px", "py"))
    shape = jax.ShapeDtypeStruct

    elems = in_hbm(sample_elems.reshape(1, samples))
    width = LANES * FACE_TILES
    tiles = slot_count // width
    piece = (3, 48, LANES)

    up, down, left, right, faces = pl.pallas_call(
        functools.partial(pack_kernel, slot_faces),
        grid=(1,),
        in_specs=[
            pl.BlockSpec((NODES, 4, reach), lambda t: (0, 0, 0)),
            fixed((4, slot_count)),
            fixed((256, ROWS)),
        ],
        out_specs=[
            fixed(piece),
            fixed(piece),
            fixed(piece[1:]),
            fixed(piece[1:]),
            fixed((slot_faces // LANES, LANES)),
        ],
        out_shape=[
            pltpu.HBM(piece, f32),
            pltpu.HBM(piece, f32),
            shape(piece[1:], f32),
            shape(piece[1:], f32),
            pltpu.HBM((slot_faces // LANES, LANES), jnp.int32),
        ],
        scratch_shapes=[pltpu.VMEM((reach // LANES, ROWS, LANES), f32)],
        compiler_params=pltpu.CompilerParams(vmem_limit_bytes=16 << 20),
        name="pack",
    )(fields, neighbours, const["trace_select"])

    def steps_along(axis):
        count = lax.axis_size(axis)
        forward = [(i, i + 1) for i in range(count - 1)]
        return forward, [(target, source) for source, target in forward]

    forward, backward = steps_along("px")
    below = lax.ppermute(up, "px", backward)
    above = lax.ppermute(down, "px", forward)
    bulk = 3 * width
    bulks = slot_count // bulk

    def behind(rank):
        return lambda t, *_: (0,) * rank + (jnp.maximum(t - bulks - 1, 0),)

    def ahead(rank):
        return lambda t, *_: (0,) * rank + (jnp.clip(t - bulks, 0, tiles - 1),)

    fields_next, residue_next, partial = pl.pallas_call(
        functools.partial(section_kernel, slot_count, reach),
        grid_spec=pltpu.PrefetchScalarGridSpec(
            num_scalar_prefetch=1,
            grid=(bulks + tiles + 1,),
            in_specs=[
                pl.BlockSpec(memory_space=pltpu.HBM),
                pl.BlockSpec((3, 4, width), ahead(2)),
                pl.BlockSpec((NODES, 4, bulk), lambda t, *_: (0, 0, jnp.minimum(t, bulks - 1))),
                pl.BlockSpec((NODES, 4, width), behind(2)),
                pl.BlockSpec((NODES, 4, width), behind(2)),
                pl.BlockSpec((9, width), behind(1)),
                pl.BlockSpec((3, 4, width), behind(2)),
                pl.BlockSpec((4, width), behind(1)),
                pl.BlockSpec((4, width), behind(1)),
                fixed((1, samples)),
                fixed((2 * ROWS, 4 * LANES)),
                fixed((256, 2 * ROWS)),
                fixed((3 * ROWS, 96)),
                fixed((ROWS, 1024)),
            ],
            out_specs=[
                pl.BlockSpec((NODES, 4, width), behind(2)),
                pl.BlockSpec((NODES, 4, width), behind(2)),
                fixed((144, samples)),
            ],
            scratch_shapes=[
                pltpu.VMEM((slot_faces, LANES), f32),
                pltpu.VMEM((width // LANES, ROWS, LANES), f32),
                pltpu.VMEM((128, width), f32),
                pltpu.VMEM((48, width), f32),
                pltpu.VMEM((ROWS, width), f32),
                pltpu.VMEM((64, width), f32),
                pltpu.VMEM((64, width), f32),
                pltpu.VMEM((48, width), f32),
                pltpu.VMEM((width // 256, 2 * ROWS, 256), bf16),
                pltpu.VMEM((width // 256, 96, 256), bf16),
                pltpu.VMEM((width // 256, 256, 256), f32),
                pltpu.VMEM((width // 256, 1024, 256), bf16),
                pltpu.SMEM((4 * width,), jnp.int32),
                pltpu.SMEM((4 * width,), jnp.int32),
                pltpu.SemaphoreType.DMA((2,)),
                *[pltpu.VMEM((LANES, LANES), f32)] * 4,
            ],
        ),
        out_shape=[
            shape(fields.shape, f32),
            shape(residue.shape, f32),
            shape((144, samples), f32),
        ],
        compiler_params=pltpu.CompilerParams(vmem_limit_bytes=48 << 20),
        name="section",
    )(
        live_counts,
        in_hbm(faces.reshape(-1)),
        normals,
        fields,
        fields,
        residue,
        geometry,
        normals,
        face_scale,
        neighbours,
        elems,
        const["table_select"],
        const["twice_select"],
        const["from_p"],
        const["lift"],
    )

    below, above, partial = lax.optimization_barrier((below, above, partial))
    to_left, to_right = pl.pallas_call(
        relay_kernel,
        out_shape=[pltpu.VMEM(piece, f32), pltpu.VMEM(piece, f32)],
        name="relay",
    )(in_vmem(left), in_vmem(right), in_vmem(below), in_vmem(above))
    forward, backward = steps_along("py")
    from_right = lax.ppermute(to_left, "py", backward)
    from_left = lax.ppermute(to_right, "py", forward)

    def head(rank):
        return lambda t: (0,) * rank

    fields_next, residue_next, spread = pl.pallas_call(
        functools.partial(boundary_kernel, slot_faces, const["powers"], samples),
        grid=(1,),
        in_specs=[
            pl.BlockSpec((NODES, 4, reach), head(3)),
            pl.BlockSpec((NODES, 4, reach), head(3)),
            pl.BlockSpec((3, 4, reach), head(3)),
            pl.BlockSpec((4, reach), head(2)),
            pl.BlockSpec((4, reach), head(2)),
            fixed(piece),
            fixed(piece),
            fixed(piece),
            fixed(piece),
            fixed((1, samples)),
            fixed((1, samples)),
            fixed((3, samples)),
            fixed((144, samples)),
            fixed((ROWS, 1024)),
            fixed((PAD, PAD)),
        ],
        out_specs=[
            pl.BlockSpec((NODES, 4, reach), head(3)),
            pl.BlockSpec((NODES, 4, reach), head(3)),
            fixed((devices, 1, samples)),
        ],
        out_shape=[
            shape(fields.shape, f32),
            shape(residue.shape, f32),
            shape((devices, 1, samples), f32),
        ],
        scratch_shapes=[
            pltpu.VMEM((64, reach), f32),
            pltpu.VMEM((768, reach), bf16),
            pltpu.VMEM((ROWS, reach), f32),
            pltpu.VMEM((48, reach), f32),
            pltpu.VMEM((PAD, samples), f32),
        ],
        input_output_aliases={0: 0, 1: 1},
        compiler_params=pltpu.CompilerParams(vmem_limit_bytes=24 << 20),
        name="boundary",
    )(
        in_hbm(fields_next),
        in_hbm(residue_next),
        normals,
        face_scale,
        neighbours,
        from_right,
        from_left,
        below,
        above,
        elems,
        in_hbm(sample_ids.reshape(1, samples)),
        sample_coords,
        partial,
        const["lift"],
        const["inverse"],
    )
    received = lax.all_to_all(spread, ("px", "py"), 0, 0, tiled=True)

    receivers = samples // QPTS
    harmonic = np.tile(harmonic_table(), (1, receivers)).astype(np.float32)
    groups = (np.arange(samples)[None] // QPTS == np.arange(receivers)[:, None]).astype(np.float32)
    coefficients = pl.pallas_call(
        harmonic_kernel,
        out_shape=shape((receivers, harmonic.shape[0]), f32),
        name="harmonic",
    )(received, jnp.asarray(harmonic), jnp.asarray(groups))
    return (
        jnp.transpose(fields_next, (1, 0, 2)),
        jnp.transpose(residue_next, (1, 0, 2)),
        coefficients.T,
    )


def solution(mesh):
    placed = (
        P(None, None, ("px", "py")),
        P(None, None, ("px", "py")),
        P(None, ("px", "py")),
        P(None, None, ("px", "py")),
        P(None, ("px", "py")),
        P(None, ("px", "py")),
        P(None, ("px", "py")),
        P(("px", "py")),
        P(("px", "py")),
        P(("px", "py")),
        P(None, ("px", "py")),
    )
    return jax.shard_map(
        local,
        mesh=mesh,
        in_specs=placed,
        out_specs=(P(None, None, ("px", "py")), P(None, None, ("px", "py")), P(None, ("px", "py"))),
        check_vma=False,
    )
```

profile of v0, /device:TPU:1, one launch (start us, length us, event | category | flops | bytes accessed | tf_op | source)
XLA Modules:
  0.0 70.8 jit_solution(609464009004541883)
XLA Ops:
  0.6 2.3 %pack.1 = (f32[3,48,128]{2,1,0:T(8,128)}, f32[3,48,128]{2,1,0:T(8,128)}, f32[48,128]{1,0:T(8,128)S(1)}, f32[48,128]{1,0:T(8,128)S(1)}, s32[144,128]{1,0:T(8,128)}) custom-call(f32[35,4,4608]{2,1,0:T(4,128)} %bitcast.8, s32[4,4608]{1,0:T(4,128)} %codes_ref.5, bf16[256,144]{1,0:T(8,128)(2,1)} %constant.17.clone.select_ref), custom_call_target="tpu_custom_call" | custom-call | tf_op jit(solution)/shard_map/pack/pallas_call | solution.py:761
  3.0 3.3 %collective-permute-start = (f32[3,48,128]{2,1,0:T(8,128)}, f32[3,48,128]{2,1,0:T(8,128)S(1)}, u32[]{:S(2)}, u32[]{:S(2)}) collective-permute-start(f32[3,48,128]{2,1,0:T(8,128)} %get-tuple-element.24), channel_id=1, source_target_pairs={{16,0},{32,16},{48,32},{64,48},{80,64},{96,80},{112,96},{17,1},{33... | collective-permute-start | bytes 221192 | tf_op jit(solution)/shard_map/ppermute | solution.py:794
  6.3 3.1 %collective-permute-start.1 = (f32[3,48,128]{2,1,0:T(8,128)}, f32[3,48,128]{2,1,0:T(8,128)S(1)}, u32[]{:S(2)}, u32[]{:S(2)}) collective-permute-start(f32[3,48,128]{2,1,0:T(8,128)} %get-tuple-element.25), channel_id=1, source_target_pairs={{0,16},{16,32},{32,48},{48,64},{64,80},{80,96},{96,112},{1,17},{17... | collective-permute-start | bytes 221192 | tf_op jit(solution)/shard_map/ppermute | solution.py:795
  10.0 18.7 %section.1 = (f32[35,4,4608]{2,1,0:T(4,128)}, f32[35,4,4608]{2,1,0:T(4,128)}, f32[144,200]{1,0:T(8,128)S(1)}) custom-call(s32[1]{0:T(128)S(6)} %copy.25.live_ref, s32[18432]{0:T(1024)} %bitcast.14, f32[3,4,4608]{2,1,0:T(4,128)} %normals_ref.3, f32[35,4,4608]{2,1,0:T(4,128)} %bitcast.9, f32[35,4,4608]{2,1,0:T(4,128)} %bitcast.10, f32[35,4,4608]{2,1,0:T(4,128)} %bitcast.13, ...), custom_call_target="tpu_custom_call" | custom-call | tf_op jit(solution)/shard_map/section/pallas_call | solution.py:805
  28.8 0.0 collective-permute-done.below_ref
  28.8 0.0 collective-permute-done.1.above_ref
  28.8 1.3 %collective-permute-start.2 = (f32[3,48,128]{2,1,0:T(8,128)S(1)}, f32[3,48,128]{2,1,0:T(8,128)S(1)}, u32[]{:S(2)}, u32[]{:S(2)}) collective-permute-start(f32[3,48,128]{2,1,0:T(8,128)S(1)} %get-tuple-element.29), channel_id=1, source_target_pairs={{1,0},{2,1},{3,2},{4,3},{5,4},{6,5},{7,6},{8,7},{9,8},{10,9},{11,1... | collective-permute-start | bytes 221192 | tf_op jit(solution)/shard_map/ppermute | solution.py:882
  30.1 4.0 %collective-permute-start.3 = (f32[3,48,128]{2,1,0:T(8,128)S(1)}, f32[3,48,128]{2,1,0:T(8,128)S(1)}, u32[]{:S(2)}, u32[]{:S(2)}) collective-permute-start(f32[3,48,128]{2,1,0:T(8,128)S(1)} %get-tuple-element.30), channel_id=1, source_target_pairs={{0,1},{1,2},{2,3},{3,4},{4,5},{5,6},{6,7},{7,8},{8,9},{9,10},{10,1... | collective-permute-start | bytes 221192 | tf_op jit(solution)/shard_map/ppermute | solution.py:883
  34.1 0.0 collective-permute-done.2.right_ref
  34.1 1.4 %collective-permute-done.3.left_ref = f32[3,48,128]{2,1,0:T(8,128)S(1)} collective-permute-done((f32[3,48,128]{2,1,0:T(8,128)S(1)}, f32[3,48,128]{2,1,0:T(8,128)S(1)}, u32[]{:S(2)}, u32[]{:S(2)}) %collective-permute-start.3) | collective-permute-done | bytes 73760 | tf_op jit(solution)/shard_map/ppermute | solution.py:883
  35.5 3.0 %boundary.1 = (f32[35,4,4608]{2,1,0:T(4,128)}, f32[35,4,4608]{2,1,0:T(4,128)}, f32[128,1,200]{2,1,0:T(1,128)S(1)}) custom-call(f32[35,4,4608]{2,1,0:T(4,128)} %get-tuple-element.20.fields_ref, f32[35,4,4608]{2,1,0:T(4,128)} %get-tuple-element.21.residue_ref, f32[3,4,4608]{2,1,0:T(4,128)} %normals_ref.3, ...), custom_call_target="tpu_custom_call", output_to_operand_aliasing={{0}: (0, {}), {1}: (1, {})} | custom-call | tf_op jit(solution)/shard_map/boundary/pallas_call | solution.py:888
  38.5 30.6 %all_to_all.5.received_ref = f32[128,1,200]{2,1,0:T(1,128)} all-to-all(f32[128,1,200]{2,1,0:T(1,128)S(1)} %get-tuple-element.34), channel_id=1, replica_groups=mesh['px'=8,'py'=16] {'px','py'}, dimensions={0} | all-to-all | bytes 204800 | tf_op jit(solution)/shard_map/all_to_all | solution.py:945
  69.0 1.8 %harmonic.1 = f32[4,25]{1,0:T(4,128)} custom-call(f32[128,1,200]{2,1,0:T(1,128)} %all_to_all.5.received_ref, f32[25,200]{1,0:T(8,128)} %constant.22.clone.table_ref, f32[4,200]{1,0:T(4,128)} %constant.23.clone.groups_ref), custom_call_target="tpu_custom_call" | custom-call | tf_op jit(solution)/shard_map/harmonic/pallas_call | solution.py:950
  (1 shorter events, 0.0 us)
Async XLA Ops:
  3.0 25.8 %collective-permute-start = (f32[3,48,128]{2,1,0:T(8,128)}, f32[3,48,128]{2,1,0:T(8,128)S(1)}, u32[]{:S(2)}, u32[]{:S(2)}) collective-permute-start(f32[3,48,128]{2,1,0:T(8,128)} %get-tuple-element.24), channel_id=1, source_target_pairs={{16,0},{32,16},{48,32},{64,48},{80,64},{96,80},{112,96},{17,1},{33... | collective-permute-start | bytes 221192 | tf_op jit(solution)/shard_map/ppermute | solution.py:794
  6.3 22.5 %collective-permute-start.1 = (f32[3,48,128]{2,1,0:T(8,128)}, f32[3,48,128]{2,1,0:T(8,128)S(1)}, u32[]{:S(2)}, u32[]{:S(2)}) collective-permute-start(f32[3,48,128]{2,1,0:T(8,128)} %get-tuple-element.25), channel_id=1, source_target_pairs={{0,16},{16,32},{32,48},{48,64},{64,80},{80,96},{96,112},{1,17},{17... | collective-permute-start | bytes 221192 | tf_op jit(solution)/shard_map/ppermute | solution.py:795
  28.8 5.3 %collective-permute-start.2 = (f32[3,48,128]{2,1,0:T(8,128)S(1)}, f32[3,48,128]{2,1,0:T(8,128)S(1)}, u32[]{:S(2)}, u32[]{:S(2)}) collective-permute-start(f32[3,48,128]{2,1,0:T(8,128)S(1)} %get-tuple-element.29), channel_id=1, source_target_pairs={{1,0},{2,1},{3,2},{4,3},{5,4},{6,5},{7,6},{8,7},{9,8},{10,9},{11,1... | collective-permute-start | bytes 221192 | tf_op jit(solution)/shard_map/ppermute | solution.py:882
  30.1 5.4 %collective-permute-start.3 = (f32[3,48,128]{2,1,0:T(8,128)S(1)}, f32[3,48,128]{2,1,0:T(8,128)S(1)}, u32[]{:S(2)}, u32[]{:S(2)}) collective-permute-start(f32[3,48,128]{2,1,0:T(8,128)S(1)} %get-tuple-element.30), channel_id=1, source_target_pairs={{0,1},{1,2},{2,3},{3,4},{4,5},{5,6},{6,7},{7,8},{8,9},{9,10},{10,1... | collective-permute-start | bytes 221192 | tf_op jit(solution)/shard_map/ppermute | solution.py:883
where the time goes:
time: 72 us; the launch traced here: 70.8 us
  blocking collectives  30.6 us (42%)
  Pallas kernels  25.8 us (36%)
  starting transfers between devices  11.7 us (16%)
  waiting for transfers between devices  1.38 us (2%)
  between operations  1.35 us (2%)
    all_to_all x1, blocking collectives, local(): received = lax.all_to_all(spread, ('px', 'py'), 0, 0, tiled=True)  30.6 us
    pallas_call x1, Pallas kernels, local(): pl.pallas_call(functools.partial(section_kernel, slot_count, reach), grid...  18.7 us
    ppermute x1, starting transfers between devices, local(): from_left = lax.ppermute(to_right, 'py', forward)  3.99 us
    ppermute x1, starting transfers between devices, local(): below = lax.ppermute(up, 'px', backward)  3.32 us
    ppermute x1, starting transfers between devices, local(): above = lax.ppermute(down, 'px', forward)  3.1 us
    pallas_call x1, Pallas kernels, local(): pl.pallas_call(functools.partial(boundary_kernel, slot_faces, const['powe...  2.97 us
    pallas_call x1, Pallas kernels, local(): pl.pallas_call(functools.partial(pack_kernel, slot_faces), grid=(1,), in_...  2.33 us
    pallas_call x1, Pallas kernels, local(): pl.pallas_call(harmonic_kernel, out_shape=shape((receivers, harmonic.shap...  1.79 us
  transfers between devices with their start and end apart: 4, of which 1 were waited for; matrix products, arithmetic and copies ran while one was open for 0% of the time, Pallas kernels for 26%

commit v1 on v0

--- a/solution.py
+++ b/solution.py
@@ -774,8 +774,8 @@
             fixed((slot_faces // LANES, LANES)),
         ],
         out_shape=[
-            pltpu.HBM(piece, f32),
-            pltpu.HBM(piece, f32),
+            pltpu.VMEM(piece, f32),
+            pltpu.VMEM(piece, f32),
             shape(piece[1:], f32),
             shape(piece[1:], f32),
             pltpu.HBM((slot_faces // LANES, LANES), jnp.int32),
@@ -951,7 +951,7 @@
         harmonic_kernel,
         out_shape=shape((receivers, harmonic.shape[0]), f32),
         name="harmonic",
-    )(received, jnp.asarray(harmonic), jnp.asarray(groups))
+    )(in_vmem(received), in_vmem(jnp.asarray(harmonic)), in_vmem(jnp.asarray(groups)))
     return (
         jnp.transpose(fields_next, (1, 0, 2)),
         jnp.transpose(residue_next, (1, 0, 2)),

time: 72 us -> 72.4 us (level); the launches traced: 70.8 us -> 72 us
  Pallas kernels: 25.8 us -> 28.3 us
  blocking collectives: 30.6 us -> 29.3 us
    pallas_call x1, Pallas kernels: 18.7 us -> 22.2 us  [local(): pl.pallas_call(functools.partial(section_kernel, slot_count, reach), grid...]
    all_to_all x1, blocking collectives: 30.6 us -> 29.3 us  [local(): received = lax.all_to_all(spread, ('px', 'py'), 0, 0, tiled=True)]
    pallas_call x1, Pallas kernels: 1.79 us -> 0.87 us  [local(): pl.pallas_call(harmonic_kernel, out_shape=shape((receivers, harmonic.shap...]
  transfers between devices with their start and end apart: 4 -> 4, of which waited for: 1 -> 1; matrix products, arithmetic and copies ran while one was open for 0% -> 0% of each run, Pallas kernels for 26% -> 31%
where the time goes in v1:
time: 72.4 us; the launch traced here: 72 us
  blocking collectives  29.3 us (40%)
  Pallas kernels  28.3 us (39%)
  starting transfers between devices  11.7 us (16%)
  waiting for transfers between devices  1.38 us (2%)
  between operations  1.35 us (2%)
    all_to_all x1, blocking collectives, local(): received = lax.all_to_all(spread, ('px', 'py'), 0, 0, tiled=True)  29.3 us
    pallas_call x1, Pallas kernels, local(): pl.pallas_call(functools.partial(section_kernel, slot_count, reach), grid...  22.2 us
    ppermute x1, starting transfers between devices, local(): from_left = lax.ppermute(to_right, 'py', forward)  3.99 us
    ppermute x1, starting transfers between devices, local(): below = lax.ppermute(up, 'px', backward)  3.32 us
    ppermute x1, starting transfers between devices, local(): above = lax.ppermute(down, 'px', forward)  3.1 us
    pallas_call x1, Pallas kernels, local(): pl.pallas_call(functools.partial(boundary_kernel, slot_faces, const['powe...  2.98 us
    pallas_call x1, Pallas kernels, local(): pl.pallas_call(functools.partial(pack_kernel, slot_faces), grid=(1,), in_...  2.25 us
  transfers between devices with their start and end apart: 4, of which 1 were waited for; matrix products, arithmetic and copies ran while one was open for 0% of the time, Pallas kernels for 31%

profile of v1, /device:TPU:1, one launch (start us, length us, event | category | flops | bytes accessed | tf_op | source)
XLA Modules:
  0.0 72.0 jit_solution(4790929340171505227)
XLA Ops:
  0.6 2.2 %pack.1 = (f32[3,48,128]{2,1,0:T(8,128)S(1)}, f32[3,48,128]{2,1,0:T(8,128)S(1)}, f32[48,128]{1,0:T(8,128)S(1)}, f32[48,128]{1,0:T(8,128)S(1)}, s32[144,128]{1,0:T(8,128)}) custom-call(f32[35,4,4608]{2,1,0:T(4,128)} %bitcast.8, s32[4,4608]{1,0:T(4,128)} %codes_ref.5, bf16[256,144]{1,0:T(8,128)(2,1)} %constant.17.clone.select_ref), custom_call_target="tpu_custom_call" | custom-call | tf_op jit(solution)/shard_map/pack/pallas_call | solution.py:761
  2.9 3.3 %collective-permute-start = (f32[3,48,128]{2,1,0:T(8,128)S(1)}, f32[3,48,128]{2,1,0:T(8,128)S(1)}, u32[]{:S(2)}, u32[]{:S(2)}) collective-permute-start(f32[3,48,128]{2,1,0:T(8,128)S(1)} %get-tuple-element.24), channel_id=1, source_target_pairs={{16,0},{32,16},{48,32},{64,48},{80,64},{96,80},{112,96},{17,1},{33... | collective-permute-start | bytes 221192 | tf_op jit(solution)/shard_map/ppermute | solution.py:794
  6.2 3.1 %collective-permute-start.1 = (f32[3,48,128]{2,1,0:T(8,128)S(1)}, f32[3,48,128]{2,1,0:T(8,128)S(1)}, u32[]{:S(2)}, u32[]{:S(2)}) collective-permute-start(f32[3,48,128]{2,1,0:T(8,128)S(1)} %get-tuple-element.25), channel_id=1, source_target_pairs={{0,16},{16,32},{32,48},{48,64},{64,80},{80,96},{96,112},{1,17},{17... | collective-permute-start | bytes 221192 | tf_op jit(solution)/shard_map/ppermute | solution.py:795
  10.0 22.2 %section.1 = (f32[35,4,4608]{2,1,0:T(4,128)}, f32[35,4,4608]{2,1,0:T(4,128)}, f32[144,200]{1,0:T(8,128)S(1)}) custom-call(s32[1]{0:T(128)S(6)} %copy.25.live_ref, s32[18432]{0:T(1024)} %bitcast.14, f32[3,4,4608]{2,1,0:T(4,128)} %normals_ref.3, f32[35,4,4608]{2,1,0:T(4,128)} %bitcast.9, f32[35,4,4608]{2,1,0:T(4,128)} %bitcast.10, f32[35,4,4608]{2,1,0:T(4,128)} %bitcast.13, ...), custom_call_target="tpu_custom_call" | custom-call | tf_op jit(solution)/shard_map/section/pallas_call | solution.py:805
  32.2 0.0 collective-permute-done.below_ref
  32.2 0.0 collective-permute-done.1.above_ref
  32.2 1.3 %collective-permute-start.2 = (f32[3,48,128]{2,1,0:T(8,128)S(1)}, f32[3,48,128]{2,1,0:T(8,128)S(1)}, u32[]{:S(2)}, u32[]{:S(2)}) collective-permute-start(f32[3,48,128]{2,1,0:T(8,128)S(1)} %get-tuple-element.29), channel_id=1, source_target_pairs={{1,0},{2,1},{3,2},{4,3},{5,4},{6,5},{7,6},{8,7},{9,8},{10,9},{11,1... | collective-permute-start | bytes 221192 | tf_op jit(solution)/shard_map/ppermute | solution.py:882
  33.5 4.0 %collective-permute-start.3 = (f32[3,48,128]{2,1,0:T(8,128)S(1)}, f32[3,48,128]{2,1,0:T(8,128)S(1)}, u32[]{:S(2)}, u32[]{:S(2)}) collective-permute-start(f32[3,48,128]{2,1,0:T(8,128)S(1)} %get-tuple-element.30), channel_id=1, source_target_pairs={{0,1},{1,2},{2,3},{3,4},{4,5},{5,6},{6,7},{7,8},{8,9},{9,10},{10,1... | collective-permute-start | bytes 221192 | tf_op jit(solution)/shard_map/ppermute | solution.py:883
  37.5 0.0 collective-permute-done.2.right_ref
  37.5 1.4 %collective-permute-done.3.left_ref = f32[3,48,128]{2,1,0:T(8,128)S(1)} collective-permute-done((f32[3,48,128]{2,1,0:T(8,128)S(1)}, f32[3,48,128]{2,1,0:T(8,128)S(1)}, u32[]{:S(2)}, u32[]{:S(2)}) %collective-permute-start.3) | collective-permute-done | bytes 73760 | tf_op jit(solution)/shard_map/ppermute | solution.py:883
  38.9 0.0 copy-start
  38.9 0.0 copy-start.1
  38.9 3.0 %boundary.1 = (f32[35,4,4608]{2,1,0:T(4,128)}, f32[35,4,4608]{2,1,0:T(4,128)}, f32[128,1,200]{2,1,0:T(1,128)S(1)}) custom-call(f32[35,4,4608]{2,1,0:T(4,128)} %get-tuple-element.20.fields_ref, f32[35,4,4608]{2,1,0:T(4,128)} %get-tuple-element.21.residue_ref, f32[3,4,4608]{2,1,0:T(4,128)} %normals_ref.3, ...), custom_call_target="tpu_custom_call", output_to_operand_aliasing={{0}: (0, {}), {1}: (1, {})} | custom-call | tf_op jit(solution)/shard_map/boundary/pallas_call | solution.py:888
  41.9 29.3 %all_to_all.5.received_ref = f32[128,1,200]{2,1,0:T(1,128)S(1)} all-to-all(f32[128,1,200]{2,1,0:T(1,128)S(1)} %get-tuple-element.34), channel_id=1, replica_groups=mesh['px'=8,'py'=16] {'px','py'}, dimensions={0} | all-to-all | bytes 204800 | tf_op jit(solution)/shard_map/all_to_all | solution.py:945
  71.2 0.0 copy-done
  71.2 0.0 copy-done.1
  71.2 0.9 %harmonic.1 = f32[4,25]{1,0:T(4,128)} custom-call(f32[128,1,200]{2,1,0:T(1,128)S(1)} %all_to_all.5.received_ref, f32[25,200]{1,0:T(8,128)S(1)} %copy-done, f32[4,200]{1,0:T(4,128)S(1)} %copy-done.1), custom_call_target="tpu_custom_call" | custom-call | tf_op jit(solution)/shard_map/harmonic/pallas_call | solution.py:950
  (1 shorter events, 0.0 us)
Async XLA Ops:
  2.9 29.3 %collective-permute-start = (f32[3,48,128]{2,1,0:T(8,128)S(1)}, f32[3,48,128]{2,1,0:T(8,128)S(1)}, u32[]{:S(2)}, u32[]{:S(2)}) collective-permute-start(f32[3,48,128]{2,1,0:T(8,128)S(1)} %get-tuple-element.24), channel_id=1, source_target_pairs={{16,0},{32,16},{48,32},{64,48},{80,64},{96,80},{112,96},{17,1},{33... | collective-permute-start | bytes 221192 | tf_op jit(solution)/shard_map/ppermute | solution.py:794
  6.2 26.0 %collective-permute-start.1 = (f32[3,48,128]{2,1,0:T(8,128)S(1)}, f32[3,48,128]{2,1,0:T(8,128)S(1)}, u32[]{:S(2)}, u32[]{:S(2)}) collective-permute-start(f32[3,48,128]{2,1,0:T(8,128)S(1)} %get-tuple-element.25), channel_id=1, source_target_pairs={{0,16},{16,32},{32,48},{48,64},{64,80},{80,96},{96,112},{1,17},{17... | collective-permute-start | bytes 221192 | tf_op jit(solution)/shard_map/ppermute | solution.py:795
  32.2 5.3 %collective-permute-start.2 = (f32[3,48,128]{2,1,0:T(8,128)S(1)}, f32[3,48,128]{2,1,0:T(8,128)S(1)}, u32[]{:S(2)}, u32[]{:S(2)}) collective-permute-start(f32[3,48,128]{2,1,0:T(8,128)S(1)} %get-tuple-element.29), channel_id=1, source_target_pairs={{1,0},{2,1},{3,2},{4,3},{5,4},{6,5},{7,6},{8,7},{9,8},{10,9},{11,1... | collective-permute-start | bytes 221192 | tf_op jit(solution)/shard_map/ppermute | solution.py:882
  33.5 5.4 %collective-permute-start.3 = (f32[3,48,128]{2,1,0:T(8,128)S(1)}, f32[3,48,128]{2,1,0:T(8,128)S(1)}, u32[]{:S(2)}, u32[]{:S(2)}) collective-permute-start(f32[3,48,128]{2,1,0:T(8,128)S(1)} %get-tuple-element.30), channel_id=1, source_target_pairs={{0,1},{1,2},{2,3},{3,4},{4,5},{5,6},{6,7},{7,8},{8,9},{9,10},{10,1... | collective-permute-start | bytes 221192 | tf_op jit(solution)/shard_map/ppermute | solution.py:883
  38.9 32.3 %copy-start = (f32[25,200]{1,0:T(8,128)S(1)}, f32[25,200]{1,0:T(8,128)}, u32[]{:S(2)}) copy-start(f32[25,200]{1,0:T(8,128)} %constant.22.clone.table_ref) | copy-start | bytes 60004
  38.9 32.3 %copy-start.1 = (f32[4,200]{1,0:T(4,128)S(1)}, f32[4,200]{1,0:T(4,128)}, u32[]{:S(2)}) copy-start(f32[4,200]{1,0:T(4,128)} %constant.23.clone.groups_ref) | copy-start | bytes 9604
